TPU v7x, 512 devices: a whole 4x8x8 slice. The times are simulated.
512 devices in a mesh: pipe: 32 (over z, y_hi), expert: 16 (over y_lo, x, core).
Axes of the slice: x: 4, y: 8 (y_hi: 4, y_lo: 2; y = y_hi * 2 + y_lo), z: 8, core: 2. Of those that a mesh axis runs over, the one named last changes fastest.
Arguments:
- tokens: bfloat16 [65536, 2048], P(('pipe', 'expert')), may hold values from -6 to 6
- cotangent: bfloat16 [65536, 2048], P(('pipe', 'expert')), may hold values from -6 to 6
- chosen: int32 [512, 64, 2], P(('pipe', 'expert')), may hold values from 0 to 127, as said below
- gate_value: bfloat16 [512, 64, 2], P(('pipe', 'expert')), may hold values from 0.049804688 to 1
- gate_weight: bfloat16 [2048, 65536], P(None, ('pipe', 'expert')), may hold values from -0.125 to 0.125
- up_weight: bfloat16 [2048, 65536], P(None, ('pipe', 'expert')), may hold values from -0.125 to 0.125
- down_weight: bfloat16 [65536, 2048], P(('pipe', 'expert')), may hold values from -0.1875 to 0.1875
Outputs:
- token_grad: bfloat16 [65536, 2048], P(('pipe', 'expert'))
- gate_grad: float32 [512, 64, 2], P(('pipe', 'expert'))
- gate_weight_grad: bfloat16 [2048, 65536], P(None, ('pipe', 'expert'))
- up_weight_grad: bfloat16 [2048, 65536], P(None, ('pipe', 'expert'))
- down_weight_grad: bfloat16 [65536, 2048], P(('pipe', 'expert'))
Inputs may be any that keep to these rules, and one draw needn't show every extreme that they name: `chosen`: for each routing group and expert, the 2 entries are different token indices within that group's 128 tokens.
All inputs are finite; a program needn't handle non-finite values.
Results may differ from a plain program's by a relative error of at most 0.0095.
Values may be sent and summed in bfloat16 or wider, within the bound.
No kernel may reach another device: no remote copies, remote signals or barrier semaphores. Data moves between devices by JAX's collectives and lax.ppermute only.
A program may use at most 128 MiB of HBM per device.

v0:
```python
import functools

import jax
import jax.numpy as jnp
from jax import lax
from jax.experimental import pallas as pl
from jax.experimental.pallas import tpu as pltpu
from jax.sharding import Mesh, PartitionSpec as P

AXES = ("z", "yh", "yl", "x", "c")
ZY = ("z", "yh", "yl")
F32 = jnp.float32
BF16 = jnp.bfloat16
PAD = 128


CONTRACT_ROWS = (((0,), (0,)), ((), ()))
CONTRACT_LAST = (((1,), (1,)), ((), ()))


def call(body, out_shape):
    return pl.pallas_call(
        body, out_shape=out_shape, compiler_params=pltpu.CompilerParams(vmem_limit_bytes=48 << 20)
    )


def forward_body(*refs):
    pieces, (weights, gate_out, up_out) = refs[:-3], refs[-3:]
    half = weights.shape[1] // 2
    for i, piece in enumerate(pieces):
        n = piece.shape[0]
        pre = jnp.dot(piece[...], weights[...], preferred_element_type=F32)
        gate_out[i * n : (i + 1) * n, :] = pre[:, :half]
        up_out[i * n : (i + 1) * n, :] = pre[:, half:]


def forward(pieces, weights):
    rows = sum(p.shape[0] for p in pieces)
    shape = jax.ShapeDtypeStruct((rows, weights.shape[1] // 2), F32)
    return call(forward_body, (shape, shape))(*pieces, weights)


def backward_body(part, *refs):
    count = len(refs) - 7
    pieces = refs[:count]
    gate_ref, up_ref, weights, down, grad_out, hidden_out, both_out = refs[count:]
    features = down.shape[1]
    for i, piece in enumerate(pieces):
        n = piece.shape[0]
        span = slice(i * n, (i + 1) * n)
        source = slice((part + i) * n, (part + i + 1) * n)
        gate_pre = gate_ref[source, :]
        up_pre = up_ref[source, :]
        hidden_grad = lax.dot_general(
            piece[...], down[...], CONTRACT_LAST, preferred_element_type=F32
        )
        logistic = 1.0 / (1.0 + jnp.exp(-gate_pre))
        activated = gate_pre * logistic
        hidden = (activated * up_pre).astype(BF16)
        router = jnp.sum(hidden.astype(F32) * hidden_grad, axis=1, keepdims=True)
        gate_grad = (
            hidden_grad * up_pre * logistic * (1.0 + gate_pre * (1.0 - logistic))
        ).astype(BF16)
        up_grad = (hidden_grad * activated).astype(BF16)
        both = jnp.concatenate([gate_grad, up_grad], axis=1)
        hidden_out[span, :] = hidden
        both_out[span, :] = both
        grad_out[span, :features] = lax.dot_general(
            both, weights[...], CONTRACT_LAST, preferred_element_type=F32
        ).astype(BF16)
        grad_out[span, features:] = jnp.broadcast_to(router, (n, PAD)).astype(BF16)


def backward(pieces, part, pre, weights, down):
    rows = sum(p.shape[0] for p in pieces)
    width, features = down.shape
    out = (
        jax.ShapeDtypeStruct((rows, features + PAD), BF16),
        jax.ShapeDtypeStruct((rows, width), BF16),
        jax.ShapeDtypeStruct((rows, 2 * width), BF16),
    )
    body = functools.partial(backward_body, part)
    return call(body, out)(*pieces, *pre, weights, down)


def weights_body(count, *refs):
    xs, dys = refs[:count], refs[count : 2 * count]
    rest = refs[2 * count :]
    groups = (len(rest) - 4) // 2
    hiddens, boths = rest[:groups], rest[groups : 2 * groups]
    mine_up, mine_down, send_up, send_down = rest[2 * groups :]
    features, width = send_up.shape[0] // 2, send_up.shape[1]
    x = jnp.concatenate([r[...] for r in xs], axis=0)
    both = jnp.concatenate([r[...] for r in boths], axis=0)
    grads = lax.dot_general(x, both, CONTRACT_ROWS, preferred_element_type=F32)
    mine_up[:features, :] = grads[:, :width]
    send_up[:features, :] = grads[:, width : 2 * width].astype(BF16)
    mine_up[features:, :] = grads[:, 2 * width : 3 * width]
    send_up[features:, :] = grads[:, 3 * width :].astype(BF16)
    dy = jnp.concatenate([r[...] for r in dys], axis=0)
    hidden = jnp.concatenate([r[...] for r in hiddens], axis=0)
    down = lax.dot_general(hidden, dy, CONTRACT_ROWS, preferred_element_type=F32)
    mine_down[...] = down[:width, :]
    send_down[...] = down[width:, :].astype(BF16)


def weight_grads(xs, dys, hiddens, boths):
    features, width = xs[0].shape[1], hiddens[0].shape[1] // 2
    out = (
        jax.ShapeDtypeStruct((2 * features, width), F32),
        jax.ShapeDtypeStruct((width, features), F32),
        jax.ShapeDtypeStruct((2 * features, width), BF16),
        jax.ShapeDtypeStruct((width, features), BF16),
    )
    body = functools.partial(weights_body, len(xs))
    return call(body, out)(*xs, *dys, *hiddens, *boths)


def add(a, b):
    return a.astype(F32) + b.astype(F32)


def near(value):
    return lax.ppermute(value, "x", [(i, i ^ 1) for i in range(4)])


def across(value):
    return lax.ppermute(value, "x", [(i, 3 - i) for i in range(4)])


def swap(value):
    return lax.ppermute(value, "c", [(0, 1), (1, 0)])


def exchange(value):
    return lax.all_to_all(value, ZY, split_axis=0, concat_axis=0, tiled=True)


def per_device(tokens, cotangent, chosen, gate_value, wg, wu, wd):
    tok, features = tokens.shape
    experts, picks = chosen.shape[1:]
    slots = experts * picks
    listed = chosen[0].reshape(-1)
    factor = gate_value[0].reshape(-1).astype(F32)[:, None]
    onehot = (listed[:, None] == jnp.arange(tok, dtype=jnp.int32)[None, :]).astype(BF16)
    x_rows = jnp.dot(onehot, tokens, preferred_element_type=F32).astype(BF16)
    dy_rows = (factor * jnp.dot(onehot, cotangent, preferred_element_type=F32)).astype(BF16)
    cut = (experts, picks, features)
    got = exchange(jnp.concatenate([x_rows.reshape(cut), dy_rows.reshape(cut)], axis=1))
    x_own = got[:, :picks].reshape(slots, features)
    dy_own = got[:, picks:].reshape(slots, features)

    wgu_near = near(jnp.concatenate([wg, wu], axis=0))
    down = jnp.concatenate([wd, near(wd)], axis=0)
    weights = jnp.concatenate([wg, wgu_near[:features], wu, wgu_near[features:]], axis=1)

    x_far, dy_far = across(x_own), across(dy_own)
    x_other, dy_other = swap(x_own), swap(dy_own)
    x_cross, dy_cross = swap(x_far), swap(dy_far)

    pre = forward([x_own, x_other], weights)
    grad, hid_a, both_a = backward([dy_own, dy_other], 0, pre, weights, down)
    keep = add(grad[:slots], swap(grad[slots:]))
    pre = forward([x_far, x_cross], weights)
    grad_cross, hid_c, both_c = backward([dy_cross], 1, pre, weights, down)
    theirs = swap(grad_cross)
    grad_far, hid_b, both_b = backward([dy_far], 0, pre, weights, down)
    arrived = across(add(grad_far, theirs).astype(BF16))
    total = add(keep, arrived).astype(BF16)
    home = exchange(total.reshape(experts, picks, -1)).reshape(slots, -1)

    mine_up, mine_down, send_up, send_down = weight_grads(
        [x_own, x_other, x_far, x_cross],
        [dy_own, dy_other, dy_far, dy_cross],
        [hid_a, hid_b, hid_c],
        [both_a, both_b, both_c],
    )
    up = near(send_up)
    dwg = add(mine_up[:features], up[:features]).astype(BF16)
    dwu = add(mine_up[features:], up[features:]).astype(BF16)
    dwd = add(mine_down, near(send_down)).astype(BF16)
    token_grad = lax.dot_general(
        onehot, home[:, :features], CONTRACT_ROWS, preferred_element_type=F32
    ).astype(BF16)
    gate_grad = (home[:, features : features + 1].astype(F32) / factor).reshape(1, experts, picks)
    return token_grad, gate_grad, dwg, dwu, dwd


def solution(mesh):
    grid = Mesh(mesh.devices.reshape(8, 4, 2, 4, 2), AXES)
    rows, cols = P(AXES, None), P(None, AXES)
    lists = P(AXES, None, None)
    return jax.shard_map(
        per_device,
        mesh=grid,
        in_specs=(rows, rows, lists, lists, cols, cols, rows),
        out_specs=(rows, lists, cols, cols, rows),
        check_vma=False,
    )
```

profile of v0, /device:TPU:24, one launch (start us, length us, event | category | flops | bytes accessed | tf_op | source)
XLA Modules:
  0.0 153.7 jit_solution(4355787607230428418)
XLA Ops:
  0.6 0.0 copy-start
  0.7 0.8 copy.18
  1.5 0.1 reshape.54
  1.6 0.8 copy.17
  2.4 0.1 eq.15
  2.6 0.3 fusion
  2.9 0.3 reshape.48
  3.3 0.3 convolution_convert_fusion.1
  3.6 0.3 reshape.47
  4.0 0.0 copy-start.2
  4.0 0.0 copy-start.3
  4.0 2.1 %pad_maximum_fusion.1 = bf16[64,4,2048]{2,1,0:T(4,128)(2,1)} fusion(bf16[64,2,2048]{2,1,0:T(2,128)(2,1)S(1)} %reshape.48, bf16[64,2,2048]{2,1,0:T(2,128)(2,1)S(1)} %reshape.47), kind=kLoop, calls=%fused_computation.7 | loop fusion | flops 2097152 | bytes 2097152 | tf_op jit(solution)/shard_map/concatenate | solution.py:149
  6.1 16.4 %all-to-all-start = ((bf16[64,4,2048]{2,1,0:T(4,128)(2,1)}), bf16[64,4,2048]{2,1,0:T(4,128)(2,1)S(1)}, u32[]{:S(2)}, u32[]{:S(2)}) async-start(bf16[64,4,2048]{2,1,0:T(4,128)(2,1)} %pad_maximum_fusion.1), calls=%async_computation | async-start | bytes 2097152 | tf_op jit(solution)/shard_map/all_to_all | solution.py:136
  22.4 1.1 pad_maximum_fusion.2
  23.5 3.4 %collective-permute-start.2 = (bf16[4096,128]{1,0:T(8,128)(2,1)}, bf16[4096,128]{1,0:T(8,128)(2,1)}, u32[]{:S(2)}, u32[]{:S(2)}) collective-permute-start(bf16[4096,128]{1,0:T(8,128)(2,1)} %pad_maximum_fusion.2), channel_id=1, source_target_pairs={{0,2},{2,0},{4,6},{6,4},{1,3},{3,1},{5,7},{7,5},{8,10},{10,8},{12,... | collective-permute-start | bytes 3145736 | tf_op jit(solution)/shard_map/ppermute | solution.py:124
  26.9 2.4 %collective-permute-start.3 = (bf16[128,2048]{1,0:T(8,128)(2,1)}, bf16[128,2048]{1,0:T(8,128)(2,1)}, u32[]{:S(2)}, u32[]{:S(2)}) collective-permute-start(bf16[128,2048]{1,0:T(8,128)(2,1)} %param.13), channel_id=1, source_target_pairs={{0,2},{2,0},{4,6},{6,4},{1,3},{3,1},{5,7},{7,5},{8,10},{10,8},{12,... | collective-permute-start | bytes 1572872 | tf_op jit(solution)/shard_map/ppermute | solution.py:124
  29.3 22.4 %all-to-all-done = bf16[64,4,2048]{2,1,0:T(4,128)(2,1)S(1)} async-done(((bf16[64,4,2048]{2,1,0:T(4,128)(2,1)}), bf16[64,4,2048]{2,1,0:T(4,128)(2,1)S(1)}, u32[]{:S(2)}, u32[]{:S(2)}) %all-to-all-start) | async-done | bytes 1048608 | tf_op jit(solution)/shard_map/all_to_all | solution.py:136
  51.8 0.7 fusion.7
  52.5 0.2 reshape.49.refs_0_.refs_4_
  52.7 4.7 %collective-permute-start.5 = (bf16[128,2048]{1,0:T(8,128)(2,1)S(1)}, bf16[128,2048]{1,0:T(8,128)(2,1)S(1)}, u32[]{:S(2)}, u32[]{:S(2)}) collective-permute-start(bf16[128,2048]{1,0:T(8,128)(2,1)S(1)} %reshape.49.refs_0_.refs_4_), channel_id=1, source_target_pairs={{0,6},{2,4},{4,2},{6,0},{1,7},{3,5},{5,3},{7,1},{8,14},{10,12},{12... | collective-permute-start | bytes 1572872 | tf_op jit(solution)/shard_map/ppermute | solution.py:128
  57.4 0.2 reshape.50.refs_0_
  57.6 0.0 copy-start.4
  57.6 2.5 %collective-permute-start.6 = (bf16[128,2048]{1,0:T(8,128)(2,1)S(1)}, bf16[128,2048]{1,0:T(8,128)(2,1)S(1)}, u32[]{:S(2)}, u32[]{:S(2)}) collective-permute-start(bf16[128,2048]{1,0:T(8,128)(2,1)S(1)} %reshape.50.refs_0_), channel_id=1, source_target_pairs={{0,6},{2,4},{4,2},{6,0},{1,7},{3,5},{5,3},{7,1},{8,14},{10,12},{12... | collective-permute-start | bytes 1572872 | tf_op jit(solution)/shard_map/ppermute | solution.py:128
  60.1 1.1 constant_dynamic-update-slice_fusion.1
  61.2 0.1 collective-permute-done.3
  61.3 1.1 constant_dynamic-update-slice_fusion.refs_5_.refs_4_
  62.4 8.3 %collective-permute-done.5.refs_0_.refs_6_ = bf16[128,2048]{1,0:T(8,128)(2,1)S(1)} collective-permute-done((bf16[128,2048]{1,0:T(8,128)(2,1)S(1)}, bf16[128,2048]{1,0:T(8,128)(2,1)S(1)}, u32[]{:S(2)}, u32[]{:S(2)}) %collective-permute-start.5) | collective-permute-done | bytes 524320 | tf_op jit(solution)/shard_map/ppermute | solution.py:128
  70.6 1.9 %collective-permute-start.8 = (bf16[128,2048]{1,0:T(8,128)(2,1)S(1)}, bf16[128,2048]{1,0:T(8,128)(2,1)S(1)}, u32[]{:S(2)}, u32[]{:S(2)}) collective-permute-start(bf16[128,2048]{1,0:T(8,128)(2,1)S(1)} %collective-permute-done.5.refs_0_.refs_6_), channel_id=1, source_target_pairs={{0,1},{1,0},{2,3},{3,2},{4,5},{5,4},{6,7},{7,6},{8,9},{9,8},{10,11... | collective-permute-start | bytes 1572872 | tf_op jit(solution)/shard_map/ppermute | solution.py:132
  72.5 6.7 %collective-permute-done.6.refs_0_.refs_2_ = bf16[128,2048]{1,0:T(8,128)(2,1)S(1)} collective-permute-done((bf16[128,2048]{1,0:T(8,128)(2,1)S(1)}, bf16[128,2048]{1,0:T(8,128)(2,1)S(1)}, u32[]{:S(2)}, u32[]{:S(2)}) %collective-permute-start.6) | collective-permute-done | bytes 524320 | tf_op jit(solution)/shard_map/ppermute | solution.py:128
  79.3 1.9 %collective-permute-start.7 = (bf16[128,2048]{1,0:T(8,128)(2,1)S(1)}, bf16[128,2048]{1,0:T(8,128)(2,1)S(1)}, u32[]{:S(2)}, u32[]{:S(2)}) collective-permute-start(bf16[128,2048]{1,0:T(8,128)(2,1)S(1)} %collective-permute-done.6.refs_0_.refs_2_), channel_id=1, source_target_pairs={{0,1},{1,0},{2,3},{3,2},{4,5},{5,4},{6,7},{7,6},{8,9},{9,8},{10,11... | collective-permute-start | bytes 1572872 | tf_op jit(solution)/shard_map/ppermute | solution.py:132
  81.2 1.3 fusion.6
  82.5 0.2 pad_maximum_fusion.refs_2_.refs_4_.refs_3_
  82.7 0.3 collective-permute-done.7.refs_1_.refs_3_
  83.1 0.7 shard_map.112
  83.8 0.0 collective-permute-done.8.refs_0_.refs_7_
  83.8 1.7 %shard_map.114 = (bf16[128,2176]{1,0:T(8,128)(2,1)S(1)}, bf16[128,256]{1,0:T(8,128)(2,1)S(1)}, bf16[128,512]{1,0:T(8,128)(2,1)S(1)}) custom-call(bf16[128,2048]{1,0:T(8,128)(2,1)S(1)} %collective-permute-done.8.refs_0_.refs_7_, f32[256,256]{1,0:T(8,128)S(1)} %get-tuple-element.25.refs_1_, f32[256,256]{1,0:T(8,128)S(1)} %get-tuple-element.26.refs_2_, ...), custom_call_target="tpu_custom_call" | custom-call | tf_op jit(solution)/shard_map/pallas_call | solution.py:83
  85.5 2.1 %collective-permute-start.9 = (bf16[128,2176]{1,0:T(8,128)(2,1)S(1)}, bf16[128,2176]{1,0:T(8,128)(2,1)S(1)}, u32[]{:S(2)}, u32[]{:S(2)}) collective-permute-start(bf16[128,2176]{1,0:T(8,128)(2,1)S(1)} %get-tuple-element.28), channel_id=1, source_target_pairs={{0,1},{1,0},{2,3},{3,2},{4,5},{5,4},{6,7},{7,6},{8,9},{9,8},{10,11... | collective-permute-start | bytes 1671176 | tf_op jit(solution)/shard_map/ppermute | solution.py:132
  87.5 2.3 %collective-permute-start.1 = (bf16[128,2048]{1,0:T(8,128)(2,1)S(1)}, bf16[128,2048]{1,0:T(8,128)(2,1)S(1)}, u32[]{:S(2)}, u32[]{:S(2)}) collective-permute-start(bf16[128,2048]{1,0:T(8,128)(2,1)S(1)} %reshape.50.refs_0_), channel_id=1, source_target_pairs={{0,1},{1,0},{2,3},{3,2},{4,5},{5,4},{6,7},{7,6},{8,9},{9,8},{10,11... | collective-permute-start | bytes 1572872 | tf_op jit(solution)/shard_map/ppermute | solution.py:132
  89.8 2.1 %collective-permute-start = (bf16[128,2048]{1,0:T(8,128)(2,1)S(1)}, bf16[128,2048]{1,0:T(8,128)(2,1)S(1)}, u32[]{:S(2)}, u32[]{:S(2)}) collective-permute-start(bf16[128,2048]{1,0:T(8,128)(2,1)S(1)} %reshape.49.refs_0_.refs_4_), channel_id=1, source_target_pairs={{0,1},{1,0},{2,3},{3,2},{4,5},{5,4},{6,7},{7,6},{8,9},{9,8},{10,11... | collective-permute-start | bytes 1572872 | tf_op jit(solution)/shard_map/ppermute | solution.py:132
  91.9 0.0 collective-permute-done.1.refs_1_
  91.9 0.7 shard_map.110
  92.6 1.0 collective-permute-done.refs_1_.refs_5_
  93.6 2.7 %shard_map.111 = (bf16[256,2176]{1,0:T(8,128)(2,1)S(1)}, bf16[256,256]{1,0:T(8,128)(2,1)S(1)}, bf16[256,512]{1,0:T(8,128)(2,1)S(1)}) custom-call(bf16[128,2048]{1,0:T(8,128)(2,1)S(1)} %reshape.49.refs_0_.refs_4_, bf16[128,2048]{1,0:T(8,128)(2,1)S(1)} %collective-permute-done.refs_1_.refs_5_, f32[256,256]{1,0:T(8,128)S(1)} %get-tuple-element.22.refs_2_, ...), custom_call_target="tpu_custom_call" | custom-call | tf_op jit(solution)/shard_map/pallas_call | solution.py:83
  96.4 2.1 %collective-permute-start.4 = (bf16[128,2176]{1,0:T(8,128)(2,1)S(1)}, bf16[128,2176]{1,0:T(8,128)(2,1)S(1)}, u32[]{:S(2)}, u32[]{:S(2)}) collective-permute-start(bf16[128,2176]{1,0:T(8,128)(2,1)S(1)} %slice.41), channel_id=1, source_target_pairs={{0,1},{1,0},{2,3},{3,2},{4,5},{5,4},{6,7},{7,6},{8,9},{9,8},{10,11... | collective-permute-start | bytes 1671176 | tf_op jit(solution)/shard_map/ppermute | solution.py:132
  98.5 1.7 %shard_map.113 = (bf16[128,2176]{1,0:T(8,128)(2,1)S(1)}, bf16[128,256]{1,0:T(8,128)(2,1)S(1)}, bf16[128,512]{1,0:T(8,128)(2,1)S(1)}) custom-call(bf16[128,2048]{1,0:T(8,128)(2,1)S(1)} %collective-permute-done.5.refs_0_.refs_6_, f32[256,256]{1,0:T(8,128)S(1)} %get-tuple-element.25.refs_1_, f32[256,256]{1,0:T(8,128)S(1)} %get-tuple-element.26.refs_2_, ...), custom_call_target="tpu_custom_call" | custom-call | tf_op jit(solution)/shard_map/pallas_call | solution.py:83
  100.1 0.1 add_convert_fusion.1
  100.3 4.8 %collective-permute-start.10 = (bf16[128,2176]{1,0:T(8,128)(2,1)S(1)}, bf16[128,2176]{1,0:T(8,128)(2,1)S(1)}, u32[]{:S(2)}, u32[]{:S(2)}) collective-permute-start(bf16[128,2176]{1,0:T(8,128)(2,1)S(1)} %add_convert_fusion.1), channel_id=1, source_target_pairs={{0,6},{2,4},{4,2},{6,0},{1,7},{3,5},{5,3},{7,1},{8,14},{10,12},{12... | collective-permute-start | bytes 1671176 | tf_op jit(solution)/shard_map/ppermute | solution.py:128
  105.1 3.2 %shard_map.115 = (f32[4096,128]{1,0:T(8,128)}, f32[128,2048]{1,0:T(8,128)}, bf16[4096,128]{1,0:T(8,128)(2,1)}, bf16[128,2048]{1,0:T(8,128)(2,1)S(1)}) custom-call(bf16[128,2048]{1,0:T(8,128)(2,1)S(1)} %reshape.50.refs_0_, bf16[128,2048]{1,0:T(8,128)(2,1)S(1)} %collective-permute-done.1.refs_1_, bf16[128,2048]{1,0:T(8,128)(2,1)S(1)} %collective-permute-done.6.refs_0_.refs_2_, ...), custom_call_target="tpu_custom_call" | custom-call | tf_op jit(solution)/shard_map/pallas_call | solution.py:116
  108.4 1.9 %collective-permute-start.11 = (bf16[4096,128]{1,0:T(8,128)(2,1)}, bf16[4096,128]{1,0:T(8,128)(2,1)}, u32[]{:S(2)}, u32[]{:S(2)}) collective-permute-start(bf16[4096,128]{1,0:T(8,128)(2,1)} %get-tuple-element.36), channel_id=1, source_target_pairs={{0,2},{2,0},{4,6},{6,4},{1,3},{3,1},{5,7},{7,5},{8,10},{10,8},{12,... | collective-permute-start | bytes 3145736 | tf_op jit(solution)/shard_map/ppermute | solution.py:124
  110.3 3.9 %collective-permute-start.12 = (bf16[128,2048]{1,0:T(8,128)(2,1)S(1)}, bf16[128,2048]{1,0:T(8,128)(2,1)S(1)}, u32[]{:S(2)}, u32[]{:S(2)}) collective-permute-start(bf16[128,2048]{1,0:T(8,128)(2,1)S(1)} %get-tuple-element.38), channel_id=1, source_target_pairs={{0,2},{2,0},{4,6},{6,4},{1,3},{3,1},{5,7},{7,5},{8,10},{10,8},{12,... | collective-permute-start | bytes 1572872 | tf_op jit(solution)/shard_map/ppermute | solution.py:124
  114.2 4.0 %collective-permute-done.10 = bf16[128,2176]{1,0:T(8,128)(2,1)S(1)} collective-permute-done((bf16[128,2176]{1,0:T(8,128)(2,1)S(1)}, bf16[128,2176]{1,0:T(8,128)(2,1)S(1)}, u32[]{:S(2)}, u32[]{:S(2)}) %collective-permute-start.10) | collective-permute-done | bytes 557088 | tf_op jit(solution)/shard_map/ppermute | solution.py:128
  118.3 0.2 add_convert_fusion
  118.5 1.0 reshape.51
  119.5 7.3 %all-to-all-start.1 = ((bf16[64,2,2176]{2,1,0:T(2,128)(2,1)}), bf16[64,2,2176]{2,1,0:T(2,128)(2,1)S(1)}, u32[]{:S(2)}, u32[]{:S(2)}) async-start(bf16[64,2,2176]{2,1,0:T(2,128)(2,1)} %reshape.51), calls=%async_computation.1 | async-start | bytes 1114112 | tf_op jit(solution)/shard_map/all_to_all | solution.py:136
  126.8 0.1 reshape.56
  126.9 19.9 %collective-permute-done.12 = bf16[128,2048]{1,0:T(8,128)(2,1)S(1)} collective-permute-done((bf16[128,2048]{1,0:T(8,128)(2,1)S(1)}, bf16[128,2048]{1,0:T(8,128)(2,1)S(1)}, u32[]{:S(2)}, u32[]{:S(2)}) %collective-permute-start.12) | collective-permute-done | bytes 524320 | tf_op jit(solution)/shard_map/ppermute | solution.py:124
  146.8 2.1 %add_convert_fusion.2 = bf16[128,2048]{1,0:T(8,128)(2,1)} fusion(f32[128,2048]{1,0:T(8,128)} %get-tuple-element.37, bf16[128,2048]{1,0:T(8,128)(2,1)S(1)} %collective-permute-done.12), kind=kLoop, calls=%fused_computation.9 | loop fusion | flops 786432 | bytes 2097152 | tf_op jit(solution)/shard_map/convert_element_type | solution.py:181
  149.0 0.0 collective-permute-done.11
  149.0 2.4 %add_convert_fusion.3 = (bf16[2048,128]{1,0:T(8,128)(2,1)}, bf16[2048,128]{1,0:T(8,128)(2,1)}) fusion(f32[4096,128]{1,0:T(8,128)S(1)} %copy-done.1, bf16[4096,128]{1,0:T(8,128)(2,1)} %collective-permute-done.11), kind=kLoop, calls=%fused_computation.10 | loop fusion | flops 1572864 | bytes 4194304 | tf_op jit(solution)/shard_map/convert_element_type | solution.py:180
  151.4 0.2 reshape.52
  151.6 1.2 convolution_convert_fusion
  152.8 0.1 fusion.2
  152.9 0.1 reshape.53
  153.1 0.6 copy.21
  (13 shorter events, 0.1 us)
Async XLA Ops:
  0.6 1.9 %copy-start = (bf16[128,2048]{1,0:T(8,128)(2,1)S(1)}, bf16[128,2048]{1,0:T(8,128)(2,1)}, u32[]{:S(2)}) copy-start(bf16[128,2048]{1,0:T(8,128)(2,1)} %param.8) | copy-start | bytes 1572868
  0.6 2.6 %copy-start.5 = (bf16[128,2048]{1,0:T(8,128)(2,1)S(1)}, bf16[128,2048]{1,0:T(8,128)(2,1)}, u32[]{:S(2)}) copy-start(bf16[128,2048]{1,0:T(8,128)(2,1)} %param.7) | copy-start | bytes 1572868
  4.0 18.5 %copy-start.2 = (bf16[2048,128]{1,0:T(8,128)(2,1)S(1)}, bf16[2048,128]{1,0:T(8,128)(2,1)}, u32[]{:S(2)}) copy-start(bf16[2048,128]{1,0:T(8,128)(2,1)} %param.12) | copy-start | bytes 1572868
  4.0 18.5 %copy-start.3 = (bf16[2048,128]{1,0:T(8,128)(2,1)S(1)}, bf16[2048,128]{1,0:T(8,128)(2,1)}, u32[]{:S(2)}) copy-start(bf16[2048,128]{1,0:T(8,128)(2,1)} %param.11) | copy-start | bytes 1572868
  6.1 45.7 %all-to-all-start = ((bf16[64,4,2048]{2,1,0:T(4,128)(2,1)}), bf16[64,4,2048]{2,1,0:T(4,128)(2,1)S(1)}, u32[]{:S(2)}, u32[]{:S(2)}) async-start(bf16[64,4,2048]{2,1,0:T(4,128)(2,1)} %pad_maximum_fusion.1), calls=%async_computation | async-start | bytes 2097152 | tf_op jit(solution)/shard_map/all_to_all | solution.py:136
  23.5 57.7 %collective-permute-start.2 = (bf16[4096,128]{1,0:T(8,128)(2,1)}, bf16[4096,128]{1,0:T(8,128)(2,1)}, u32[]{:S(2)}, u32[]{:S(2)}) collective-permute-start(bf16[4096,128]{1,0:T(8,128)(2,1)} %pad_maximum_fusion.2), channel_id=1, source_target_pairs={{0,2},{2,0},{4,6},{6,4},{1,3},{3,1},{5,7},{7,5},{8,10},{10,8},{12,... | collective-permute-start | bytes 3145736 | tf_op jit(solution)/shard_map/ppermute | solution.py:124
  26.9 34.4 %collective-permute-start.3 = (bf16[128,2048]{1,0:T(8,128)(2,1)}, bf16[128,2048]{1,0:T(8,128)(2,1)}, u32[]{:S(2)}, u32[]{:S(2)}) collective-permute-start(bf16[128,2048]{1,0:T(8,128)(2,1)} %param.13), channel_id=1, source_target_pairs={{0,2},{2,0},{4,6},{6,4},{1,3},{3,1},{5,7},{7,5},{8,10},{10,8},{12,... | collective-permute-start | bytes 1572872 | tf_op jit(solution)/shard_map/ppermute | solution.py:124
  52.7 17.9 %collective-permute-start.5 = (bf16[128,2048]{1,0:T(8,128)(2,1)S(1)}, bf16[128,2048]{1,0:T(8,128)(2,1)S(1)}, u32[]{:S(2)}, u32[]{:S(2)}) collective-permute-start(bf16[128,2048]{1,0:T(8,128)(2,1)S(1)} %reshape.49.refs_0_.refs_4_), channel_id=1, source_target_pairs={{0,6},{2,4},{4,2},{6,0},{1,7},{3,5},{5,3},{7,1},{8,14},{10,12},{12... | collective-permute-start | bytes 1572872 | tf_op jit(solution)/shard_map/ppermute | solution.py:128
  57.6 24.9 %copy-start.4 = (bf16[2048,128]{1,0:T(8,128)(2,1)S(1)}, bf16[2048,128]{1,0:T(8,128)(2,1)}, u32[]{:S(2)}) copy-start(bf16[2048,128]{1,0:T(8,128)(2,1)} %param.11) | copy-start | bytes 1572868
  57.6 21.7 %collective-permute-start.6 = (bf16[128,2048]{1,0:T(8,128)(2,1)S(1)}, bf16[128,2048]{1,0:T(8,128)(2,1)S(1)}, u32[]{:S(2)}, u32[]{:S(2)}) collective-permute-start(bf16[128,2048]{1,0:T(8,128)(2,1)S(1)} %reshape.50.refs_0_), channel_id=1, source_target_pairs={{0,6},{2,4},{4,2},{6,0},{1,7},{3,5},{5,3},{7,1},{8,14},{10,12},{12... | collective-permute-start | bytes 1572872 | tf_op jit(solution)/shard_map/ppermute | solution.py:128
  70.6 13.2 %collective-permute-start.8 = (bf16[128,2048]{1,0:T(8,128)(2,1)S(1)}, bf16[128,2048]{1,0:T(8,128)(2,1)S(1)}, u32[]{:S(2)}, u32[]{:S(2)}) collective-permute-start(bf16[128,2048]{1,0:T(8,128)(2,1)S(1)} %collective-permute-done.5.refs_0_.refs_6_), channel_id=1, source_target_pairs={{0,1},{1,0},{2,3},{3,2},{4,5},{5,4},{6,7},{7,6},{8,9},{9,8},{10,11... | collective-permute-start | bytes 1572872 | tf_op jit(solution)/shard_map/ppermute | solution.py:132
  79.3 3.8 %collective-permute-start.7 = (bf16[128,2048]{1,0:T(8,128)(2,1)S(1)}, bf16[128,2048]{1,0:T(8,128)(2,1)S(1)}, u32[]{:S(2)}, u32[]{:S(2)}) collective-permute-start(bf16[128,2048]{1,0:T(8,128)(2,1)S(1)} %collective-permute-done.6.refs_0_.refs_2_), channel_id=1, source_target_pairs={{0,1},{1,0},{2,3},{3,2},{4,5},{5,4},{6,7},{7,6},{8,9},{9,8},{10,11... | collective-permute-start | bytes 1572872 | tf_op jit(solution)/shard_map/ppermute | solution.py:132
  85.5 14.7 %collective-permute-start.9 = (bf16[128,2176]{1,0:T(8,128)(2,1)S(1)}, bf16[128,2176]{1,0:T(8,128)(2,1)S(1)}, u32[]{:S(2)}, u32[]{:S(2)}) collective-permute-start(bf16[128,2176]{1,0:T(8,128)(2,1)S(1)} %get-tuple-element.28), channel_id=1, source_target_pairs={{0,1},{1,0},{2,3},{3,2},{4,5},{5,4},{6,7},{7,6},{8,9},{9,8},{10,11... | collective-permute-start | bytes 1671176 | tf_op jit(solution)/shard_map/ppermute | solution.py:132
  87.5 4.3 %collective-permute-start.1 = (bf16[128,2048]{1,0:T(8,128)(2,1)S(1)}, bf16[128,2048]{1,0:T(8,128)(2,1)S(1)}, u32[]{:S(2)}, u32[]{:S(2)}) collective-permute-start(bf16[128,2048]{1,0:T(8,128)(2,1)S(1)} %reshape.50.refs_0_), channel_id=1, source_target_pairs={{0,1},{1,0},{2,3},{3,2},{4,5},{5,4},{6,7},{7,6},{8,9},{9,8},{10,11... | collective-permute-start | bytes 1572872 | tf_op jit(solution)/shard_map/ppermute | solution.py:132
  89.8 3.8 %collective-permute-start = (bf16[128,2048]{1,0:T(8,128)(2,1)S(1)}, bf16[128,2048]{1,0:T(8,128)(2,1)S(1)}, u32[]{:S(2)}, u32[]{:S(2)}) collective-permute-start(bf16[128,2048]{1,0:T(8,128)(2,1)S(1)} %reshape.49.refs_0_.refs_4_), channel_id=1, source_target_pairs={{0,1},{1,0},{2,3},{3,2},{4,5},{5,4},{6,7},{7,6},{8,9},{9,8},{10,11... | collective-permute-start | bytes 1572872 | tf_op jit(solution)/shard_map/ppermute | solution.py:132
  96.4 17.8 %collective-permute-start.4 = (bf16[128,2176]{1,0:T(8,128)(2,1)S(1)}, bf16[128,2176]{1,0:T(8,128)(2,1)S(1)}, u32[]{:S(2)}, u32[]{:S(2)}) collective-permute-start(bf16[128,2176]{1,0:T(8,128)(2,1)S(1)} %slice.41), channel_id=1, source_target_pairs={{0,1},{1,0},{2,3},{3,2},{4,5},{5,4},{6,7},{7,6},{8,9},{9,8},{10,11... | collective-permute-start | bytes 1671176 | tf_op jit(solution)/shard_map/ppermute | solution.py:132
  100.3 18.0 %collective-permute-start.10 = (bf16[128,2176]{1,0:T(8,128)(2,1)S(1)}, bf16[128,2176]{1,0:T(8,128)(2,1)S(1)}, u32[]{:S(2)}, u32[]{:S(2)}) collective-permute-start(bf16[128,2176]{1,0:T(8,128)(2,1)S(1)} %add_convert_fusion.1), channel_id=1, source_target_pairs={{0,6},{2,4},{4,2},{6,0},{1,7},{3,5},{5,3},{7,1},{8,14},{10,12},{12... | collective-permute-start | bytes 1671176 | tf_op jit(solution)/shard_map/ppermute | solution.py:128
  108.4 40.6 %collective-permute-start.11 = (bf16[4096,128]{1,0:T(8,128)(2,1)}, bf16[4096,128]{1,0:T(8,128)(2,1)}, u32[]{:S(2)}, u32[]{:S(2)}) collective-permute-start(bf16[4096,128]{1,0:T(8,128)(2,1)} %get-tuple-element.36), channel_id=1, source_target_pairs={{0,2},{2,0},{4,6},{6,4},{1,3},{3,1},{5,7},{7,5},{8,10},{10,8},{12,... | collective-permute-start | bytes 3145736 | tf_op jit(solution)/shard_map/ppermute | solution.py:124
  110.3 36.5 %collective-permute-start.12 = (bf16[128,2048]{1,0:T(8,128)(2,1)S(1)}, bf16[128,2048]{1,0:T(8,128)(2,1)S(1)}, u32[]{:S(2)}, u32[]{:S(2)}) collective-permute-start(bf16[128,2048]{1,0:T(8,128)(2,1)S(1)} %get-tuple-element.38), channel_id=1, source_target_pairs={{0,2},{2,0},{4,6},{6,4},{1,3},{3,1},{5,7},{7,5},{8,10},{10,8},{12,... | collective-permute-start | bytes 1572872 | tf_op jit(solution)/shard_map/ppermute | solution.py:124
  119.5 31.9 %all-to-all-start.1 = ((bf16[64,2,2176]{2,1,0:T(2,128)(2,1)}), bf16[64,2,2176]{2,1,0:T(2,128)(2,1)S(1)}, u32[]{:S(2)}, u32[]{:S(2)}) async-start(bf16[64,2,2176]{2,1,0:T(2,128)(2,1)} %reshape.51), calls=%async_computation.1 | async-start | bytes 1114112 | tf_op jit(solution)/shard_map/all_to_all | solution.py:136
  126.9 22.0 %copy-start.1 = (f32[4096,128]{1,0:T(8,128)S(1)}, f32[4096,128]{1,0:T(8,128)}, u32[]{:S(2)}) copy-start(f32[4096,128]{1,0:T(8,128)} %get-tuple-element.35) | copy-start | bytes 6291460
where the time goes:
time: 155 us; the launch traced here: 154 us
  waiting for transfers between devices  62.8 us (41%)
  starting transfers between devices  59.7 us (39%)
  Pallas kernels  10.7 us (7%)
  local copies, waits for them, and re-layouts  9.29 us (6%)
  other arithmetic  8.36 us (5%)
  matrix products  1.89 us (1%)
    all_to_all x2, starting transfers between devices, exchange(): return lax.all_to_all(value, ZY, split_axis=0, concat_axis=0, tiled=True)  23.7 us
    all_to_all x2, waiting for transfers between devices, exchange(): return lax.all_to_all(value, ZY, split_axis=0, concat_axis=0, tiled=True)  22.4 us
    ppermute x4, waiting for transfers between devices, near(): return lax.ppermute(value, 'x', [(i, i ^ 1) for i in range(4)])  20 us
    ppermute x3, waiting for transfers between devices, across(): return lax.ppermute(value, 'x', [(i, 3 - i) for i in range(4)])  19 us
    ppermute x6, starting transfers between devices, swap(): return lax.ppermute(value, 'c', [(0, 1), (1, 0)])  12.3 us
    ppermute x3, starting transfers between devices, across(): return lax.ppermute(value, 'x', [(i, 3 - i) for i in range(4)])  12 us
    ppermute x4, starting transfers between devices, near(): return lax.ppermute(value, 'x', [(i, i ^ 1) for i in range(4)])  11.7 us
    pallas_call x3, Pallas kernels, backward(): return call(body, out)(*pieces, *pre, weights, down)  6.02 us
  transfers between devices with their start and end apart: 15, of which 8 were waited for; matrix products, arithmetic and copies ran while one was open for 8% of the time, Pallas kernels for 6%

commit v1 on v0

--- a/solution.py
+++ b/solution.py
@@ -24,8 +24,12 @@
     )
 
 
-def forward_body(*refs):
-    pieces, (weights, gate_out, up_out) = refs[:-3], refs[-3:]
+def joined_up(wg, wu, packed):
+    n = wg.shape[0]
+    return jnp.concatenate([wg[...], packed[:n, :], wu[...], packed[n : 2 * n, :]], axis=1)
+
+
+def forward_pieces(pieces, weights, gate_out, up_out):
     half = weights.shape[1] // 2
     for i, piece in enumerate(pieces):
         n = piece.shape[0]
@@ -34,16 +38,33 @@
         up_out[i * n : (i + 1) * n, :] = pre[:, half:]
 
 
+def forward_body(*refs):
+    forward_pieces(refs[:-3], *refs[-3:])
+
+
+def forward_join_body(*refs):
+    pieces, (wg, wu, packed, gate_out, up_out, weights) = refs[:-6], refs[-6:]
+    weights[...] = joined_up(wg, wu, packed)
+    forward_pieces(pieces, weights, gate_out, up_out)
+
+
 def forward(pieces, weights):
     rows = sum(p.shape[0] for p in pieces)
     shape = jax.ShapeDtypeStruct((rows, weights.shape[1] // 2), F32)
     return call(forward_body, (shape, shape))(*pieces, weights)
 
 
-def backward_body(part, *refs):
-    count = len(refs) - 7
-    pieces = refs[:count]
-    gate_ref, up_ref, weights, down, grad_out, hidden_out, both_out = refs[count:]
+def forward_join(pieces, wg, wu, packed):
+    rows = sum(p.shape[0] for p in pieces)
+    features, width = wg.shape
+    shape = jax.ShapeDtypeStruct((rows, 2 * width), F32)
+    joined = jax.ShapeDtypeStruct((features, 4 * width), BF16)
+    return call(forward_join_body, (shape, shape, joined))(
+        *pieces, wg, wu, packed
+    )
+
+
+def backward_pieces(part, pieces, gate_ref, up_ref, weights, down, grad_out, hidden_out, both_out):
     features = down.shape[1]
     for i, piece in enumerate(pieces):
         n = piece.shape[0]
@@ -65,10 +86,31 @@
         both = jnp.concatenate([gate_grad, up_grad], axis=1)
         hidden_out[span, :] = hidden
         both_out[span, :] = both
-        grad_out[span, :features] = lax.dot_general(
-            both, weights[...], CONTRACT_LAST, preferred_element_type=F32
-        ).astype(BF16)
-        grad_out[span, features:] = jnp.broadcast_to(router, (n, PAD)).astype(BF16)
+        grad = lax.dot_general(both, weights[...], CONTRACT_LAST, preferred_element_type=F32)
+        tail = jnp.broadcast_to(router, (n, PAD))
+        if isinstance(grad_out, list):
+            out, rows = grad_out[i], slice(0, n)
+        else:
+            out, rows = grad_out, span
+        out[rows, :features] = grad.astype(BF16)
+        out[rows, features:] = tail.astype(BF16)
+
+
+def backward_body(part, *refs):
+    backward_pieces(part, refs[:-7], *refs[-7:])
+
+
+def backward_join_body(*refs):
+    dy_a, dy_b, gate_ref, up_ref, weights, wd, packed = refs[:7]
+    grad_a, grad_b, hidden_out, both_out, down = refs[7:]
+    width, features = wd.shape
+    down[:width, :] = wd[...]
+    for i in range(features // width):
+        start = 2 * features + i * width
+        down[width:, i * width : (i + 1) * width] = packed[start : start + width, :]
+    backward_pieces(
+        0, (dy_a, dy_b), gate_ref, up_ref, weights, down, [grad_a, grad_b], hidden_out, both_out
+    )
 
 
 def backward(pieces, part, pre, weights, down):
@@ -81,6 +123,21 @@
     )
     body = functools.partial(backward_body, part)
     return call(body, out)(*pieces, *pre, weights, down)
+
+
+def backward_join(dy_a, dy_b, pre, weights, wd, packed):
+    rows, (width, features) = dy_a.shape[0], wd.shape
+    grad = jax.ShapeDtypeStruct((rows, features + PAD), BF16)
+    out = (
+        grad,
+        grad,
+        jax.ShapeDtypeStruct((2 * rows, 2 * width), BF16),
+        jax.ShapeDtypeStruct((2 * rows, 4 * width), BF16),
+        jax.ShapeDtypeStruct((2 * width, features), BF16),
+    )
+    return call(backward_join_body, out)(
+        dy_a, dy_b, *pre, weights, wd, packed
+    )
 
 
 def weights_body(count, *refs):
@@ -150,17 +207,19 @@
     x_own = got[:, :picks].reshape(slots, features)
     dy_own = got[:, picks:].reshape(slots, features)
 
-    wgu_near = near(jnp.concatenate([wg, wu], axis=0))
-    down = jnp.concatenate([wd, near(wd)], axis=0)
-    weights = jnp.concatenate([wg, wgu_near[:features], wu, wgu_near[features:]], axis=1)
+    width = wd.shape[0]
+    tiles = jnp.transpose(wd.reshape(width, -1, width), (1, 0, 2)).reshape(-1, width)
+    packed = near(jnp.concatenate([wg, wu, tiles], axis=0))
 
     x_far, dy_far = across(x_own), across(dy_own)
     x_other, dy_other = swap(x_own), swap(dy_own)
     x_cross, dy_cross = swap(x_far), swap(dy_far)
 
-    pre = forward([x_own, x_other], weights)
-    grad, hid_a, both_a = backward([dy_own, dy_other], 0, pre, weights, down)
-    keep = add(grad[:slots], swap(grad[slots:]))
+    *pre, weights = forward_join([x_own, x_other], wg, wu, packed)
+    grad_own, grad_other, hid_a, both_a, down = backward_join(
+        dy_own, dy_other, pre, weights, wd, packed
+    )
+    keep = add(grad_own, swap(grad_other))
     pre = forward([x_far, x_cross], weights)
     grad_cross, hid_c, both_c = backward([dy_cross], 1, pre, weights, down)
     theirs = swap(grad_cross)

time: 155 us -> 157 us (1.013)
  Pallas kernels: 10.7 us -> 15.8 us
  starting transfers between devices: 59.7 us -> 57.4 us
  waiting for transfers between devices: 62.8 us -> 60.7 us
  local copies, waits for them, and re-layouts: 9.29 us -> 11.1 us
    pallas_call x0 -> x2, Pallas kernels: none -> 6.43 us  [the longest x1 4.47 us: backward_join(): return call(backward_join_body, out)(dy_a, dy_b, *pre, weights, wd, packed)]
    ppermute x3, waiting for transfers between devices: 19 us -> 15.1 us  [across(): return lax.ppermute(value, 'x', [(i, 3 - i) for i in range(4)])]
    pallas_call x3 -> x2, Pallas kernels: 6.02 us -> 3.32 us  [backward(): return call(body, out)(*pieces, *pre, weights, down)]
    ppermute x4 -> x3, starting transfers between devices: 11.7 us -> 9.22 us  [near(): return lax.ppermute(value, 'x', [(i, i ^ 1) for i in range(4)])]
    all_to_all x2, waiting for transfers between devices: 22.4 us -> 24.5 us  [exchange(): return lax.all_to_all(value, ZY, split_axis=0, concat_axis=0, tiled=True)]
    ppermute x4 -> x3, waiting for transfers between devices: 20 us -> 21.1 us  [near(): return lax.ppermute(value, 'x', [(i, i ^ 1) for i in range(4)])]
    unnamed x15 -> x24, local copies, waits for them, and re-layouts: 2.54 us -> 3.54 us
  transfers between devices with their start and end apart: 15 -> 14, of which waited for: 8 -> 5; matrix products, arithmetic and copies ran while one was open for 8% -> 7% of each run, Pallas kernels for 6% -> 9%
where the time goes in v1:
time: 157 us; the launch traced here: 156 us
  waiting for transfers between devices  60.7 us (39%)
  starting transfers between devices  57.4 us (37%)
  Pallas kernels  15.8 us (10%)
  local copies, waits for them, and re-layouts  11.1 us (7%)
  other arithmetic  8.2 us (5%)
  matrix products  1.89 us (1%)
    all_to_all x2, waiting for transfers between devices, exchange(): return lax.all_to_all(value, ZY, split_axis=0, concat_axis=0, tiled=True)  24.5 us
    all_to_all x2, starting transfers between devices, exchange(): return lax.all_to_all(value, ZY, split_axis=0, concat_axis=0, tiled=True)  23.8 us
    ppermute x3, waiting for transfers between devices, near(): return lax.ppermute(value, 'x', [(i, i ^ 1) for i in range(4)])  21.1 us
    ppermute x3, waiting for transfers between devices, across(): return lax.ppermute(value, 'x', [(i, 3 - i) for i in range(4)])  15.1 us
    ppermute x6, starting transfers between devices, swap(): return lax.ppermute(value, 'c', [(0, 1), (1, 0)])  12.5 us
    ppermute x3, starting transfers between devices, across(): return lax.ppermute(value, 'x', [(i, 3 - i) for i in range(4)])  11.9 us
    ppermute x3, starting transfers between devices, near(): return lax.ppermute(value, 'x', [(i, i ^ 1) for i in range(4)])  9.22 us
    pallas_call x1, Pallas kernels, backward_join(): return call(backward_join_body, out)(dy_a, dy_b, *pre, weights, wd, packed)  4.47 us
  transfers between devices with their start and end apart: 14, of which 5 were waited for; matrix products, arithmetic and copies ran while one was open for 7% of the time, Pallas kernels for 9%

profile of v1, /device:TPU:24, one launch (start us, length us, event | category | flops | bytes accessed | tf_op | source)
XLA Modules:
  0.0 156.1 jit_solution(11105342156112110747)
XLA Ops:
  0.6 0.0 copy-start
  0.7 0.8 copy.19
  1.5 0.1 reshape.62
  1.6 0.8 copy.18
  2.4 0.1 eq.15
  2.6 0.3 fusion
  2.9 0.3 reshape.54
  3.3 0.3 convolution_convert_fusion.1
  3.6 0.3 reshape.53
  4.0 0.0 copy-start.6
  4.0 2.1 %pad_maximum_fusion.1 = bf16[64,4,2048]{2,1,0:T(4,128)(2,1)} fusion(bf16[64,2,2048]{2,1,0:T(2,128)(2,1)S(1)} %reshape.54, bf16[64,2,2048]{2,1,0:T(2,128)(2,1)S(1)} %reshape.53), kind=kLoop, calls=%fused_computation.7 | loop fusion | flops 2097152 | bytes 2097152 | tf_op jit(solution)/shard_map/concatenate | solution.py:206
  6.1 16.5 %all-to-all-start = ((bf16[64,4,2048]{2,1,0:T(4,128)(2,1)}), bf16[64,4,2048]{2,1,0:T(4,128)(2,1)S(1)}, u32[]{:S(2)}, u32[]{:S(2)}) async-start(bf16[64,4,2048]{2,1,0:T(4,128)(2,1)} %pad_maximum_fusion.1), calls=%async_computation | async-start | bytes 2097152 | tf_op jit(solution)/shard_map/all_to_all | solution.py:193
  22.6 0.1 copy_bitcast_fusion
  22.7 1.3 pad_maximum_fusion
  24.0 3.4 %collective-permute-start.2 = (bf16[6144,128]{1,0:T(8,128)(2,1)}, bf16[6144,128]{1,0:T(8,128)(2,1)S(1)}, u32[]{:S(2)}, u32[]{:S(2)}) collective-permute-start(bf16[6144,128]{1,0:T(8,128)(2,1)} %pad_maximum_fusion), channel_id=1, source_target_pairs={{0,2},{2,0},{4,6},{6,4},{1,3},{3,1},{5,7},{7,5},{8,10},{10,8},{12,... | collective-permute-start | bytes 4718600 | tf_op jit(solution)/shard_map/ppermute | solution.py:181
  27.4 24.5 %all-to-all-done = bf16[64,4,2048]{2,1,0:T(4,128)(2,1)S(1)} async-done(((bf16[64,4,2048]{2,1,0:T(4,128)(2,1)}), bf16[64,4,2048]{2,1,0:T(4,128)(2,1)S(1)}, u32[]{:S(2)}, u32[]{:S(2)}) %all-to-all-start) | async-done | bytes 1048608 | tf_op jit(solution)/shard_map/all_to_all | solution.py:193
  51.9 1.7 %fusion.6 = (bf16[64,2,2048]{2,1,0:T(2,128)(2,1)}, bf16[64,2,2048]{2,1,0:T(2,128)(2,1)}) fusion(bf16[64,4,2048]{2,1,0:T(4,128)(2,1)S(1)} %all-to-all-done), kind=kLoop, calls=%fused_computation.19 | loop fusion | bytes 2097152 | tf_op jit(solution)/shard_map/slice | solution.py:207
  53.6 1.2 reshape.56.refs_0_
  54.8 4.7 %collective-permute-start.5 = (bf16[128,2048]{1,0:T(8,128)(2,1)S(1)}, bf16[128,2048]{1,0:T(8,128)(2,1)}, u32[]{:S(2)}, u32[]{:S(2)}) collective-permute-start(bf16[128,2048]{1,0:T(8,128)(2,1)S(1)} %reshape.56.refs_0_), channel_id=1, source_target_pairs={{0,6},{2,4},{4,2},{6,0},{1,7},{3,5},{5,3},{7,1},{8,14},{10,12},{12... | collective-permute-start | bytes 1572872 | tf_op jit(solution)/shard_map/ppermute | solution.py:185
  59.5 1.2 reshape.55.refs_0_.refs_4_
  60.8 2.4 %collective-permute-start.4 = (bf16[128,2048]{1,0:T(8,128)(2,1)S(1)}, bf16[128,2048]{1,0:T(8,128)(2,1)S(1)}, u32[]{:S(2)}, u32[]{:S(2)}) collective-permute-start(bf16[128,2048]{1,0:T(8,128)(2,1)S(1)} %reshape.55.refs_0_.refs_4_), channel_id=1, source_target_pairs={{0,6},{2,4},{4,2},{6,0},{1,7},{3,5},{5,3},{7,1},{8,14},{10,12},{12... | collective-permute-start | bytes 1572872 | tf_op jit(solution)/shard_map/ppermute | solution.py:185
  63.2 1.9 %collective-permute-start.1 = (bf16[128,2048]{1,0:T(8,128)(2,1)S(1)}, bf16[128,2048]{1,0:T(8,128)(2,1)S(1)}, u32[]{:S(2)}, u32[]{:S(2)}) collective-permute-start(bf16[128,2048]{1,0:T(8,128)(2,1)S(1)} %reshape.56.refs_0_), channel_id=1, source_target_pairs={{0,1},{1,0},{2,3},{3,2},{4,5},{5,4},{6,7},{7,6},{8,9},{9,8},{10,11... | collective-permute-start | bytes 1572872 | tf_op jit(solution)/shard_map/ppermute | solution.py:189
  65.1 2.4 %collective-permute-start = (bf16[128,2048]{1,0:T(8,128)(2,1)S(1)}, bf16[128,2048]{1,0:T(8,128)(2,1)S(1)}, u32[]{:S(2)}, u32[]{:S(2)}) collective-permute-start(bf16[128,2048]{1,0:T(8,128)(2,1)S(1)} %reshape.55.refs_0_.refs_4_), channel_id=1, source_target_pairs={{0,1},{1,0},{2,3},{3,2},{4,5},{5,4},{6,7},{7,6},{8,9},{9,8},{10,11... | collective-permute-start | bytes 1572872 | tf_op jit(solution)/shard_map/ppermute | solution.py:189
  67.5 5.4 %collective-permute-done.5.refs_0_.refs_2_ = bf16[128,2048]{1,0:T(8,128)(2,1)} collective-permute-done((bf16[128,2048]{1,0:T(8,128)(2,1)S(1)}, bf16[128,2048]{1,0:T(8,128)(2,1)}, u32[]{:S(2)}, u32[]{:S(2)}) %collective-permute-start.5) | collective-permute-done | bytes 524320 | tf_op jit(solution)/shard_map/ppermute | solution.py:185
  72.8 1.9 %collective-permute-start.6 = (bf16[128,2048]{1,0:T(8,128)(2,1)}, bf16[128,2048]{1,0:T(8,128)(2,1)S(1)}, u32[]{:S(2)}, u32[]{:S(2)}) collective-permute-start(bf16[128,2048]{1,0:T(8,128)(2,1)} %collective-permute-done.5.refs_0_.refs_2_), channel_id=1, source_target_pairs={{0,1},{1,0},{2,3},{3,2},{4,5},{5,4},{6,7},{7,6},{8,9},{9,8},{10,11... | collective-permute-start | bytes 1572872 | tf_op jit(solution)/shard_map/ppermute | solution.py:189
  74.8 6.6 %collective-permute-done.4.refs_0_.refs_6_ = bf16[128,2048]{1,0:T(8,128)(2,1)S(1)} collective-permute-done((bf16[128,2048]{1,0:T(8,128)(2,1)S(1)}, bf16[128,2048]{1,0:T(8,128)(2,1)S(1)}, u32[]{:S(2)}, u32[]{:S(2)}) %collective-permute-start.4) | collective-permute-done | bytes 524320 | tf_op jit(solution)/shard_map/ppermute | solution.py:185
  81.4 1.9 %collective-permute-start.7 = (bf16[128,2048]{1,0:T(8,128)(2,1)S(1)}, bf16[128,2048]{1,0:T(8,128)(2,1)S(1)}, u32[]{:S(2)}, u32[]{:S(2)}) collective-permute-start(bf16[128,2048]{1,0:T(8,128)(2,1)S(1)} %collective-permute-done.4.refs_0_.refs_6_), channel_id=1, source_target_pairs={{0,1},{1,0},{2,3},{3,2},{4,5},{5,4},{6,7},{7,6},{8,9},{9,8},{10,11... | collective-permute-start | bytes 1572872 | tf_op jit(solution)/shard_map/ppermute | solution.py:189
  83.3 0.0 collective-permute-done.2.refs_4_.refs_6_
  83.3 0.0 collective-permute-done.1.refs_1_
  83.3 0.0 copy-start.3
  83.4 1.0 copy-done.3
  84.4 1.0 copy-done.5
  85.4 2.0 %shard_map.110 = (f32[256,256]{1,0:T(8,128)S(1)}, f32[256,256]{1,0:T(8,128)S(1)}, bf16[2048,512]{1,0:T(8,128)(2,1)}) custom-call(bf16[128,2048]{1,0:T(8,128)(2,1)S(1)} %reshape.56.refs_0_, bf16[128,2048]{1,0:T(8,128)(2,1)S(1)} %collective-permute-done.1.refs_1_, bf16[2048,128]{1,0:T(8,128)(2,1)S(1)} %copy-done.3, bf16[2048,128]{1,0:T(8,128)(2,1)S(1)} %copy-done.5, ...), custom_call_target="tpu_custom_call" | custom-call | tf_op jit(solution)/shard_map/pallas_call | solution.py:62
  87.4 0.0 collective-permute-done.refs_1_.refs_5_
  87.4 4.5 %shard_map.111 = (bf16[128,2176]{1,0:T(8,128)(2,1)S(1)}, bf16[128,2176]{1,0:T(8,128)(2,1)S(1)}, bf16[256,256]{1,0:T(8,128)(2,1)S(1)}, bf16[256,512]{1,0:T(8,128)(2,1)S(1)}, bf16[256,2048]{1,0:T(8,128)(2,1)S(1)}) custom-call(bf16[128,2048]{1,0:T(8,128)(2,1)S(1)} %reshape.55.refs_0_.refs_4_, bf16[128,2048]{1,0:T(8,128)(2,1)S(1)} %collective-permute-done.refs_1_.refs_5_, ...), custom_call_target="tpu_custom_call" | custom-call | tf_op jit(solution)/shard_map/pallas_call | solution.py:138
  91.9 0.0 collective-permute-done.6.refs_1_.refs_3_
  91.9 1.8 %shard_map.112 = (f32[256,256]{1,0:T(8,128)S(1)}, f32[256,256]{1,0:T(8,128)S(1)}) custom-call(bf16[128,2048]{1,0:T(8,128)(2,1)} %collective-permute-done.5.refs_0_.refs_2_, bf16[128,2048]{1,0:T(8,128)(2,1)S(1)} %collective-permute-done.6.refs_1_.refs_3_, bf16[2048,512]{1,0:T(8,128)(2,1)S(1)} %copy-done.1), custom_call_target="tpu_custom_call" | custom-call | tf_op jit(solution)/shard_map/pallas_call | solution.py:54
  93.7 0.0 collective-permute-done.7.refs_0_.refs_7_
  93.7 1.7 %shard_map.114 = (bf16[128,2176]{1,0:T(8,128)(2,1)S(1)}, bf16[128,256]{1,0:T(8,128)(2,1)S(1)}, bf16[128,512]{1,0:T(8,128)(2,1)S(1)}) custom-call(bf16[128,2048]{1,0:T(8,128)(2,1)S(1)} %collective-permute-done.7.refs_0_.refs_7_, f32[256,256]{1,0:T(8,128)S(1)} %get-tuple-element.30.refs_1_, f32[256,256]{1,0:T(8,128)S(1)} %get-tuple-element.31.refs_2_, ...), custom_call_target="tpu_custom_call" | custom-call | tf_op jit(solution)/shard_map/pallas_call | solution.py:125
  95.3 2.4 %collective-permute-start.8 = (bf16[128,2176]{1,0:T(8,128)(2,1)S(1)}, bf16[128,2176]{1,0:T(8,128)(2,1)S(1)}, u32[]{:S(2)}, u32[]{:S(2)}) collective-permute-start(bf16[128,2176]{1,0:T(8,128)(2,1)S(1)} %get-tuple-element.34), channel_id=1, source_target_pairs={{0,1},{1,0},{2,3},{3,2},{4,5},{5,4},{6,7},{7,6},{8,9},{9,8},{10,11... | collective-permute-start | bytes 1671176 | tf_op jit(solution)/shard_map/ppermute | solution.py:189
  97.8 1.9 %collective-permute-start.3 = (bf16[128,2176]{1,0:T(8,128)(2,1)S(1)}, bf16[128,2176]{1,0:T(8,128)(2,1)S(1)}, u32[]{:S(2)}, u32[]{:S(2)}) collective-permute-start(bf16[128,2176]{1,0:T(8,128)(2,1)S(1)} %get-tuple-element.29), channel_id=1, source_target_pairs={{0,1},{1,0},{2,3},{3,2},{4,5},{5,4},{6,7},{7,6},{8,9},{9,8},{10,11... | collective-permute-start | bytes 1671176 | tf_op jit(solution)/shard_map/ppermute | solution.py:189
  99.7 1.7 %shard_map.113 = (bf16[128,2176]{1,0:T(8,128)(2,1)S(1)}, bf16[128,256]{1,0:T(8,128)(2,1)S(1)}, bf16[128,512]{1,0:T(8,128)(2,1)S(1)}) custom-call(bf16[128,2048]{1,0:T(8,128)(2,1)S(1)} %collective-permute-done.4.refs_0_.refs_6_, f32[256,256]{1,0:T(8,128)S(1)} %get-tuple-element.30.refs_1_, f32[256,256]{1,0:T(8,128)S(1)} %get-tuple-element.31.refs_2_, ...), custom_call_target="tpu_custom_call" | custom-call | tf_op jit(solution)/shard_map/pallas_call | solution.py:125
  101.4 0.0 collective-permute-done.8
  101.4 0.1 add_convert_fusion.1
  101.5 4.8 %collective-permute-start.9 = (bf16[128,2176]{1,0:T(8,128)(2,1)S(1)}, bf16[128,2176]{1,0:T(8,128)(2,1)S(1)}, u32[]{:S(2)}, u32[]{:S(2)}) collective-permute-start(bf16[128,2176]{1,0:T(8,128)(2,1)S(1)} %add_convert_fusion.1), channel_id=1, source_target_pairs={{0,6},{2,4},{4,2},{6,0},{1,7},{3,5},{5,3},{7,1},{8,14},{10,12},{12... | collective-permute-start | bytes 1671176 | tf_op jit(solution)/shard_map/ppermute | solution.py:185
  106.4 4.3 %shard_map.115 = (f32[4096,128]{1,0:T(8,128)}, f32[128,2048]{1,0:T(8,128)}, bf16[4096,128]{1,0:T(8,128)(2,1)}, bf16[128,2048]{1,0:T(8,128)(2,1)S(1)}) custom-call(bf16[128,2048]{1,0:T(8,128)(2,1)S(1)} %reshape.56.refs_0_, bf16[128,2048]{1,0:T(8,128)(2,1)S(1)} %collective-permute-done.1.refs_1_, bf16[128,2048]{1,0:T(8,128)(2,1)} %collective-permute-done.5.refs_0_.refs_2_, ...), custom_call_target="tpu_custom_call" | custom-call | tf_op jit(solution)/shard_map/pallas_call | solution.py:173
  110.7 1.9 %collective-permute-start.10 = (bf16[4096,128]{1,0:T(8,128)(2,1)}, bf16[4096,128]{1,0:T(8,128)(2,1)}, u32[]{:S(2)}, u32[]{:S(2)}) collective-permute-start(bf16[4096,128]{1,0:T(8,128)(2,1)} %get-tuple-element.42), channel_id=1, source_target_pairs={{0,2},{2,0},{4,6},{6,4},{1,3},{3,1},{5,7},{7,5},{8,10},{10,8},{12,... | collective-permute-start | bytes 3145736 | tf_op jit(solution)/shard_map/ppermute | solution.py:181
  112.6 3.9 %collective-permute-start.11 = (bf16[128,2048]{1,0:T(8,128)(2,1)S(1)}, bf16[128,2048]{1,0:T(8,128)(2,1)}, u32[]{:S(2)}, u32[]{:S(2)}) collective-permute-start(bf16[128,2048]{1,0:T(8,128)(2,1)S(1)} %get-tuple-element.44), channel_id=1, source_target_pairs={{0,2},{2,0},{4,6},{6,4},{1,3},{3,1},{5,7},{7,5},{8,10},{10,8},{12,... | collective-permute-start | bytes 1572872 | tf_op jit(solution)/shard_map/ppermute | solution.py:181
  116.5 0.0 collective-permute-done.3
  116.5 3.1 %collective-permute-done.9 = bf16[128,2176]{1,0:T(8,128)(2,1)S(1)} collective-permute-done((bf16[128,2176]{1,0:T(8,128)(2,1)S(1)}, bf16[128,2176]{1,0:T(8,128)(2,1)S(1)}, u32[]{:S(2)}, u32[]{:S(2)}) %collective-permute-start.9) | collective-permute-done | bytes 557088 | tf_op jit(solution)/shard_map/ppermute | solution.py:185
  119.6 0.2 add_convert_fusion
  119.8 1.0 reshape.59
  120.9 7.4 %all-to-all-start.1 = ((bf16[64,2,2176]{2,1,0:T(2,128)(2,1)}), bf16[64,2,2176]{2,1,0:T(2,128)(2,1)S(1)}, u32[]{:S(2)}, u32[]{:S(2)}) async-start(bf16[64,2,2176]{2,1,0:T(2,128)(2,1)} %reshape.59), calls=%async_computation.1 | async-start | bytes 1114112 | tf_op jit(solution)/shard_map/all_to_all | solution.py:193
  128.2 0.1 reshape.64
  128.3 21.1 %collective-permute-done.11 = bf16[128,2048]{1,0:T(8,128)(2,1)} collective-permute-done((bf16[128,2048]{1,0:T(8,128)(2,1)S(1)}, bf16[128,2048]{1,0:T(8,128)(2,1)}, u32[]{:S(2)}, u32[]{:S(2)}) %collective-permute-start.11) | collective-permute-done | bytes 524320 | tf_op jit(solution)/shard_map/ppermute | solution.py:181
  149.4 1.9 %add_convert_fusion.2 = bf16[128,2048]{1,0:T(8,128)(2,1)} fusion(f32[128,2048]{1,0:T(8,128)S(1)} %copy-done.9, bf16[128,2048]{1,0:T(8,128)(2,1)} %collective-permute-done.11), kind=kLoop, calls=%fused_computation.8 | loop fusion | flops 786432 | bytes 2097152 | tf_op jit(solution)/shard_map/convert_element_type | solution.py:240
  151.3 0.0 collective-permute-done.10
  151.3 2.4 %add_convert_fusion.3 = (bf16[2048,128]{1,0:T(8,128)(2,1)}, bf16[2048,128]{1,0:T(8,128)(2,1)}) fusion(f32[4096,128]{1,0:T(8,128)S(1)} %copy-done.8, bf16[4096,128]{1,0:T(8,128)(2,1)} %collective-permute-done.10), kind=kLoop, calls=%fused_computation.9 | loop fusion | flops 1572864 | bytes 4194304 | tf_op jit(solution)/shard_map/convert_element_type | solution.py:239
  153.8 0.0 all-to-all-done.1
  153.8 0.2 reshape.60
  154.0 1.2 convolution_convert_fusion
  155.2 0.1 fusion.2
  155.3 0.1 reshape.61
  155.4 0.6 copy.23
  (17 shorter events, 0.0 us)
Async XLA Ops:
  0.6 1.9 %copy-start = (bf16[128,2048]{1,0:T(8,128)(2,1)S(1)}, bf16[128,2048]{1,0:T(8,128)(2,1)}, u32[]{:S(2)}) copy-start(bf16[128,2048]{1,0:T(8,128)(2,1)} %param.8) | copy-start | bytes 1572868
  0.6 2.6 %copy-start.10 = (bf16[128,2048]{1,0:T(8,128)(2,1)S(1)}, bf16[128,2048]{1,0:T(8,128)(2,1)}, u32[]{:S(2)}) copy-start(bf16[128,2048]{1,0:T(8,128)(2,1)} %param.7) | copy-start | bytes 1572868
  4.0 18.6 %copy-start.6 = (bf16[128,2048]{1,0:T(8,128)(2,1)S(1)}, bf16[128,2048]{1,0:T(8,128)(2,1)}, u32[]{:S(2)}) copy-start(bf16[128,2048]{1,0:T(8,128)(2,1)} %refs_5_.1) | copy-start | bytes 1572868
  6.1 16.6 %copy-start.2 = (bf16[2048,128]{1,0:T(8,128)(2,1)S(1)}, bf16[2048,128]{1,0:T(8,128)(2,1)}, u32[]{:S(2)}) copy-start(bf16[2048,128]{1,0:T(8,128)(2,1)} %refs_2_.1) | copy-start | bytes 1572868
  6.1 16.7 %copy-start.4 = (bf16[2048,128]{1,0:T(8,128)(2,1)S(1)}, bf16[2048,128]{1,0:T(8,128)(2,1)}, u32[]{:S(2)}) copy-start(bf16[2048,128]{1,0:T(8,128)(2,1)} %refs_3_.1) | copy-start | bytes 1572868
  6.1 45.8 %all-to-all-start = ((bf16[64,4,2048]{2,1,0:T(4,128)(2,1)}), bf16[64,4,2048]{2,1,0:T(4,128)(2,1)S(1)}, u32[]{:S(2)}, u32[]{:S(2)}) async-start(bf16[64,4,2048]{2,1,0:T(4,128)(2,1)} %pad_maximum_fusion.1), calls=%async_computation | async-start | bytes 2097152 | tf_op jit(solution)/shard_map/all_to_all | solution.py:193
  24.0 59.3 %collective-permute-start.2 = (bf16[6144,128]{1,0:T(8,128)(2,1)}, bf16[6144,128]{1,0:T(8,128)(2,1)S(1)}, u32[]{:S(2)}, u32[]{:S(2)}) collective-permute-start(bf16[6144,128]{1,0:T(8,128)(2,1)} %pad_maximum_fusion), channel_id=1, source_target_pairs={{0,2},{2,0},{4,6},{6,4},{1,3},{3,1},{5,7},{7,5},{8,10},{10,8},{12,... | collective-permute-start | bytes 4718600 | tf_op jit(solution)/shard_map/ppermute | solution.py:181
  54.8 18.0 %collective-permute-start.5 = (bf16[128,2048]{1,0:T(8,128)(2,1)S(1)}, bf16[128,2048]{1,0:T(8,128)(2,1)}, u32[]{:S(2)}, u32[]{:S(2)}) collective-permute-start(bf16[128,2048]{1,0:T(8,128)(2,1)S(1)} %reshape.56.refs_0_), channel_id=1, source_target_pairs={{0,6},{2,4},{4,2},{6,0},{1,7},{3,5},{5,3},{7,1},{8,14},{10,12},{12... | collective-permute-start | bytes 1572872 | tf_op jit(solution)/shard_map/ppermute | solution.py:185
  60.8 20.7 %collective-permute-start.4 = (bf16[128,2048]{1,0:T(8,128)(2,1)S(1)}, bf16[128,2048]{1,0:T(8,128)(2,1)S(1)}, u32[]{:S(2)}, u32[]{:S(2)}) collective-permute-start(bf16[128,2048]{1,0:T(8,128)(2,1)S(1)} %reshape.55.refs_0_.refs_4_), channel_id=1, source_target_pairs={{0,6},{2,4},{4,2},{6,0},{1,7},{3,5},{5,3},{7,1},{8,14},{10,12},{12... | collective-permute-start | bytes 1572872 | tf_op jit(solution)/shard_map/ppermute | solution.py:185
  63.2 20.2 %collective-permute-start.1 = (bf16[128,2048]{1,0:T(8,128)(2,1)S(1)}, bf16[128,2048]{1,0:T(8,128)(2,1)S(1)}, u32[]{:S(2)}, u32[]{:S(2)}) collective-permute-start(bf16[128,2048]{1,0:T(8,128)(2,1)S(1)} %reshape.56.refs_0_), channel_id=1, source_target_pairs={{0,1},{1,0},{2,3},{3,2},{4,5},{5,4},{6,7},{7,6},{8,9},{9,8},{10,11... | collective-permute-start | bytes 1572872 | tf_op jit(solution)/shard_map/ppermute | solution.py:189
  65.1 22.3 %collective-permute-start = (bf16[128,2048]{1,0:T(8,128)(2,1)S(1)}, bf16[128,2048]{1,0:T(8,128)(2,1)S(1)}, u32[]{:S(2)}, u32[]{:S(2)}) collective-permute-start(bf16[128,2048]{1,0:T(8,128)(2,1)S(1)} %reshape.55.refs_0_.refs_4_), channel_id=1, source_target_pairs={{0,1},{1,0},{2,3},{3,2},{4,5},{5,4},{6,7},{7,6},{8,9},{9,8},{10,11... | collective-permute-start | bytes 1572872 | tf_op jit(solution)/shard_map/ppermute | solution.py:189
  72.8 19.0 %collective-permute-start.6 = (bf16[128,2048]{1,0:T(8,128)(2,1)}, bf16[128,2048]{1,0:T(8,128)(2,1)S(1)}, u32[]{:S(2)}, u32[]{:S(2)}) collective-permute-start(bf16[128,2048]{1,0:T(8,128)(2,1)} %collective-permute-done.5.refs_0_.refs_2_), channel_id=1, source_target_pairs={{0,1},{1,0},{2,3},{3,2},{4,5},{5,4},{6,7},{7,6},{8,9},{9,8},{10,11... | collective-permute-start | bytes 1572872 | tf_op jit(solution)/shard_map/ppermute | solution.py:189
  81.4 12.3 %collective-permute-start.7 = (bf16[128,2048]{1,0:T(8,128)(2,1)S(1)}, bf16[128,2048]{1,0:T(8,128)(2,1)S(1)}, u32[]{:S(2)}, u32[]{:S(2)}) collective-permute-start(bf16[128,2048]{1,0:T(8,128)(2,1)S(1)} %collective-permute-done.4.refs_0_.refs_6_), channel_id=1, source_target_pairs={{0,1},{1,0},{2,3},{3,2},{4,5},{5,4},{6,7},{7,6},{8,9},{9,8},{10,11... | collective-permute-start | bytes 1572872 | tf_op jit(solution)/shard_map/ppermute | solution.py:189
  83.3 1.0 copy-start.3
  84.4 1.0 copy-start.5
  85.4 2.0 %copy-start.7 = (bf16[128,2048]{1,0:T(8,128)(2,1)S(1)}, bf16[128,2048]{1,0:T(8,128)(2,1)}, u32[]{:S(2)}) copy-start(bf16[128,2048]{1,0:T(8,128)(2,1)} %refs_5_.1) | copy-start | bytes 1572868
  87.4 4.5 %copy-start.1 = (bf16[2048,512]{1,0:T(8,128)(2,1)S(1)}, bf16[2048,512]{1,0:T(8,128)(2,1)}, u32[]{:S(2)}) copy-start(bf16[2048,512]{1,0:T(8,128)(2,1)} %get-tuple-element.27.refs_4_.refs_2_.refs_3_) | copy-start | bytes 6291460
  95.3 6.0 %collective-permute-start.8 = (bf16[128,2176]{1,0:T(8,128)(2,1)S(1)}, bf16[128,2176]{1,0:T(8,128)(2,1)S(1)}, u32[]{:S(2)}, u32[]{:S(2)}) collective-permute-start(bf16[128,2176]{1,0:T(8,128)(2,1)S(1)} %get-tuple-element.34), channel_id=1, source_target_pairs={{0,1},{1,0},{2,3},{3,2},{4,5},{5,4},{6,7},{7,6},{8,9},{9,8},{10,11... | collective-permute-start | bytes 1671176 | tf_op jit(solution)/shard_map/ppermute | solution.py:189
  97.8 18.8 %collective-permute-start.3 = (bf16[128,2176]{1,0:T(8,128)(2,1)S(1)}, bf16[128,2176]{1,0:T(8,128)(2,1)S(1)}, u32[]{:S(2)}, u32[]{:S(2)}) collective-permute-start(bf16[128,2176]{1,0:T(8,128)(2,1)S(1)} %get-tuple-element.29), channel_id=1, source_target_pairs={{0,1},{1,0},{2,3},{3,2},{4,5},{5,4},{6,7},{7,6},{8,9},{9,8},{10,11... | collective-permute-start | bytes 1671176 | tf_op jit(solution)/shard_map/ppermute | solution.py:189
  101.5 18.1 %collective-permute-start.9 = (bf16[128,2176]{1,0:T(8,128)(2,1)S(1)}, bf16[128,2176]{1,0:T(8,128)(2,1)S(1)}, u32[]{:S(2)}, u32[]{:S(2)}) collective-permute-start(bf16[128,2176]{1,0:T(8,128)(2,1)S(1)} %add_convert_fusion.1), channel_id=1, source_target_pairs={{0,6},{2,4},{4,2},{6,0},{1,7},{3,5},{5,3},{7,1},{8,14},{10,12},{12... | collective-permute-start | bytes 1671176 | tf_op jit(solution)/shard_map/ppermute | solution.py:185
  110.7 40.7 %collective-permute-start.10 = (bf16[4096,128]{1,0:T(8,128)(2,1)}, bf16[4096,128]{1,0:T(8,128)(2,1)}, u32[]{:S(2)}, u32[]{:S(2)}) collective-permute-start(bf16[4096,128]{1,0:T(8,128)(2,1)} %get-tuple-element.42), channel_id=1, source_target_pairs={{0,2},{2,0},{4,6},{6,4},{1,3},{3,1},{5,7},{7,5},{8,10},{10,8},{12,... | collective-permute-start | bytes 3145736 | tf_op jit(solution)/shard_map/ppermute | solution.py:181
  112.6 36.8 %collective-permute-start.11 = (bf16[128,2048]{1,0:T(8,128)(2,1)S(1)}, bf16[128,2048]{1,0:T(8,128)(2,1)}, u32[]{:S(2)}, u32[]{:S(2)}) collective-permute-start(bf16[128,2048]{1,0:T(8,128)(2,1)S(1)} %get-tuple-element.44), channel_id=1, source_target_pairs={{0,2},{2,0},{4,6},{6,4},{1,3},{3,1},{5,7},{7,5},{8,10},{10,8},{12,... | collective-permute-start | bytes 1572872 | tf_op jit(solution)/shard_map/ppermute | solution.py:181
  119.8 29.5 %copy-start.9 = (f32[128,2048]{1,0:T(8,128)S(1)}, f32[128,2048]{1,0:T(8,128)}, u32[]{:S(2)}) copy-start(f32[128,2048]{1,0:T(8,128)} %get-tuple-element.43) | copy-start | bytes 3145732
  120.9 32.9 %all-to-all-start.1 = ((bf16[64,2,2176]{2,1,0:T(2,128)(2,1)}), bf16[64,2,2176]{2,1,0:T(2,128)(2,1)S(1)}, u32[]{:S(2)}, u32[]{:S(2)}) async-start(bf16[64,2,2176]{2,1,0:T(2,128)(2,1)} %reshape.59), calls=%async_computation.1 | async-start | bytes 1114112 | tf_op jit(solution)/shard_map/all_to_all | solution.py:193
  128.3 23.0 %copy-start.8 = (f32[4096,128]{1,0:T(8,128)S(1)}, f32[4096,128]{1,0:T(8,128)}, u32[]{:S(2)}) copy-start(f32[4096,128]{1,0:T(8,128)} %get-tuple-element.41) | copy-start | bytes 6291460
